TPU v7x, 256 devices: a whole 4x4x8 slice. The times are simulated.
256 devices in a mesh: wide: 32 (over y, x, core), narrow: 8 (over z).
Axes of the slice: x: 4, y: 4, z: 8, core: 2. Of those that a mesh axis runs over, the one named last changes fastest.
Arguments:
- constraint_rows: bfloat16 [512, 256, 1024], P(None, ('wide', 'narrow')), may hold values from -1 to 1
- metric: bfloat16 [1024, 1024], replicated, may hold values from -8 to 8, as said below
Outputs:
- factored: float32 [512, 256, 8, 128], P(None, 'wide', 'narrow')
Inputs may be any that keep to these rules, and one draw needn't show every extreme that they name: `metric`: symmetric and positive definite.
All inputs are finite; a program needn't handle non-finite values.
Results may differ from a plain program's by a relative error of at most 0.0052.
Values may be sent and summed in bfloat16 or wider, within the bound.
No kernel may reach another device: no remote copies, remote signals or barrier semaphores. Data moves between devices by JAX's collectives and lax.ppermute only.
A program may use at most 64 MiB of HBM per device.

v0:
```python
import jax
import jax.numpy as jnp
from jax import lax
from jax.sharding import PartitionSpec as P

P_SIZE = 1024
PB = 256
NPANEL = 2


def left_solve(factor_low, right_side):
    return jax.scipy.linalg.solve_triangular(factor_low, right_side, lower=True)


def strip_major(schur_slab, strips):
    row_count = schur_slab.shape[0]
    strip_len = schur_slab.shape[1] // strips
    reordered = schur_slab.reshape(row_count, strip_len, strips).transpose(0, 2, 1)
    return reordered.reshape(row_count, 1, strips, strip_len)


def local(constraint_rows, metric):
    groups = lax.axis_size(("wide", "narrow"))
    strips = lax.axis_size("narrow")
    row_count = constraint_rows.shape[0]
    panel_depth = P_SIZE // groups
    block_rows = PB // groups
    flat_rows = constraint_rows[:, 0, :]
    projected = jnp.dot(flat_rows, metric, preferred_element_type=jnp.float32).astype(jnp.bfloat16)
    gram_cols = jnp.einsum(
        "rn,kmn->rkm",
        projected,
        lax.all_gather(constraint_rows[:panel_depth], ("wide", "narrow"), axis=1, tiled=True),
        preferred_element_type=jnp.float32,
    )
    schur_slab = (gram_cols * gram_cols).reshape(row_count, P_SIZE)
    grid_block = lax.all_to_all(
        strip_major(schur_slab, strips), "narrow", split_axis=2, concat_axis=1, tiled=True
    )
    strip_len = P_SIZE // strips
    grid_rows = row_count * strips
    narrow_panel = PB // strips
    own_strip = lax.axis_index("narrow")
    flat_block = grid_block.reshape(grid_rows, strip_len)
    for panel_number in range(NPANEL):
        col_begin = panel_number * PB
        row_begin = col_begin // groups
        strip_begin = col_begin // strips
        strip_end = strip_begin + narrow_panel
        own_rows = flat_block.reshape(row_count, strips, strip_len)[
            row_begin : row_begin + block_rows, :, strip_begin:
        ]
        shared = lax.all_gather(own_rows, "wide", axis=1, tiled=True)
        shared = shared.reshape(PB, strip_len - strip_begin)
        diag_strip, row_strip = (
            lax.all_gather(shared[:, :narrow_panel], "narrow", axis=1, tiled=True),
            lax.all_gather(flat_block[:, strip_begin:strip_end], "narrow", axis=1, tiled=True),
        )
        diag_block = diag_strip.reshape(PB, strips, narrow_panel).transpose(0, 2, 1).reshape(PB, PB)
        panel_cols = (
            row_strip.reshape(grid_rows, strips, narrow_panel)
            .transpose(0, 2, 1)
            .reshape(grid_rows, PB)
        )
        factor_low = jnp.linalg.cholesky(diag_block)
        upper_part = left_solve(factor_low, shared[:, narrow_panel:])
        column = left_solve(factor_low, panel_cols.T).T
        trailing = flat_block[:, strip_end:] - jnp.dot(
            column, upper_part, precision=lax.Precision.HIGHEST
        )
        own_cols = lax.dynamic_index_in_dim(
            column.reshape(grid_rows, narrow_panel, strips), own_strip, 2, keepdims=False
        )
        flat_block = jnp.concatenate([flat_block[:, :strip_begin], own_cols, trailing], axis=1)
    return flat_block.reshape(row_count, strips, 1, strip_len)


def solution(mesh):
    placed = (P(None, ("wide", "narrow"), None), P())
    return jax.shard_map(
        local,
        mesh=mesh,
        in_specs=placed,
        out_specs=P(None, "wide", "narrow", None),
        check_vma=False,
    )
```

profile of v0, /device:TPU:4, one launch (start us, length us, event | category | flops | bytes accessed | tf_op | source)
XLA Modules:
  0.0 463.7 jit_solution(18273028846116087548)
XLA Ops:
  6.5 1.5 slice.104
  8.1 110.0 %all-gather.6.cloned.1.call-done = bf16[4,256,1024]{2,0,1:T(4,128)(2,1)} async-done(((bf16[4,1,1024]{2,0,1:T(4,128)(2,1)}), bf16[4,256,1024]{2,0,1:T(4,128)(2,1)}) %all-gather.6.cloned.1.call-update) | async-done | bytes 2097168 | tf_op jit(solution)/shard_map/all_gather | solution.py:33
  118.1 5.7 %fusion.8 = f32[512,4,256]{0,2,1:T(8,128)} fusion(bf16[4,256,1024]{2,0,1:T(4,128)(2,1)} %all-gather.6.cloned.1.call-done, bf16[1024,1024]{1,0:T(8,128)(2,1)S(1)} %copy-done, bf16[512,1,1024]{2,0,1:T(8,128)(2,1)} %param.5), kind=kOutput, calls=%fused_computation.22 | convolution fusion | flops 2148532224 | bytes 7340032 | tf_op jit(solution)/shard_map/rn,kmn->rkm/dot_general | solution.py:30
  123.8 2.0 copy.62
  125.8 56.3 %all_to_all.4 = f32[512,1,8,128]{3,1,0,2:T(1,128)S(1)} all-to-all(f32[512,1,8,128]{3,1,0,2:T(1,128)S(1)} %bitcast.153), channel_id=1, replica_groups=mesh['wide'=32,'narrow'=8] {'narrow'}, dimensions={2} | all-to-all | bytes 4194304 | tf_op jit(solution)/shard_map/all_to_all | solution.py:37
  182.1 1.2 copy.100
  183.4 1.4 copy.68
  184.9 1.9 slice.153
  186.8 23.0 %all-gather = f32[1,1,256,128]{3,2,1,0:T(8,128)S(1)} all-gather(f32[1,1,8,128]{3,2,1,0:T(8,128)S(1)} %bitcast.150), channel_id=2, replica_groups=mesh['wide'=32,'narrow'=8] {'wide'}, dimensions={2}, use_global_device_ids=true | all-gather | bytes 135168 | tf_op jit(solution)/shard_map/all_gather | solution.py:53
  210.1 26.7 %all_gather.23 = f32[256,256]{0,1:T(8,128)S(1)} all-gather(f32[256,32]{0,1:T(8,128)S(1)} %copy.64), channel_id=1, replica_groups=mesh['wide'=32,'narrow'=8] {'narrow'}, dimensions={1}, use_global_device_ids=true | all-gather | bytes 294912 | tf_op jit(solution)/shard_map/all_gather | solution.py:56
  237.3 11.7 %cholesky.130 = f32[128,128]{1,0:T(8,128)S(1)} custom-call(f32[128,128]{1,0:T(8,128)S(1)} %cholesky.194), custom_call_target="Cholesky" | custom-call | tf_op jit(solution)/shard_map/jit(cholesky)/cholesky | solution.py:65
  249.1 9.8 %custom-call.23 = f32[1,128,128]{1,2,0:T(8,128)S(1)} custom-call(f32[1,128,128]{2,1,0:T(8,128)S(1)} %get-tuple-element.66), custom_call_target="InvertDiagBlocksLowerTriangular" | custom-call | tf_op jit(solution)/shard_map/jit(cholesky)/cholesky | solution.py:65
  258.9 0.2 constant_dynamic-update-slice_fusion.2
  259.1 0.3 convolution_subtract_fusion.5
  259.4 11.7 %cholesky.147 = f32[128,128]{1,0:T(8,128)S(1)} custom-call(f32[128,128]{1,0:T(8,128)S(1)} %convolution_subtract_fusion.5), custom_call_target="Cholesky" | custom-call | tf_op jit(solution)/shard_map/jit(cholesky)/cholesky | solution.py:65
  271.2 0.7 compare_reduce_fusion.2
  273.2 3.9 while.6
  273.2 0.6 fusion.60
  273.8 1.3 bitcast_dynamic-update-slice_fusion.4
  275.2 0.6 fusion.60
  275.8 1.3 bitcast_dynamic-update-slice_fusion.4
  277.1 19.7 %custom-call.24 = f32[2,128,128]{1,2,0:T(8,128)S(1)} custom-call(f32[2,128,128]{2,1,0:T(8,128)S(1)} %get-tuple-element.37), custom_call_target="InvertDiagBlocksLowerTriangular" | custom-call | tf_op jit(solution)/shard_map/jit(_solve_triangular)/triangular_solve | solution.py:12
  296.8 2.1 copy.83
  298.9 0.3 fusion.24
  299.3 0.3 convolution_subtract_fusion.6
  299.8 4.6 copy.99
  304.4 1.9 fusion.4
  306.3 2.0 convolution_subtract_fusion.1
  308.3 1.9 fusion.34
  310.3 2.7 convolution_subtract_fusion.2
  313.0 1.1 copy-done.5
  314.2 0.9 slice.156
  315.1 0.9 slice.154
  316.0 24.0 %all-gather.1 = f32[256,96]{1,0:T(8,128)S(1)} all-gather(f32[8,96]{1,0:T(8,128)S(1)} %copy.73), channel_id=3, replica_groups=mesh['wide'=32,'narrow'=8] {'wide'}, dimensions={0}, use_global_device_ids=true | all-gather | bytes 101376 | tf_op jit(solution)/shard_map/all_gather | solution.py:53
  340.2 26.5 %all_gather.26 = f32[256,256]{0,1:T(8,128)S(1)} all-gather(f32[256,32]{0,1:T(8,128)S(1)} %copy.85), channel_id=1, replica_groups=mesh['wide'=32,'narrow'=8] {'narrow'}, dimensions={1}, use_global_device_ids=true | all-gather | bytes 294912 | tf_op jit(solution)/shard_map/all_gather | solution.py:56
  367.2 11.7 %cholesky.164 = f32[128,128]{1,0:T(8,128)S(1)} custom-call(f32[128,128]{1,0:T(8,128)S(1)} %cholesky.197), custom_call_target="Cholesky" | custom-call | tf_op jit(solution)/shard_map/jit(cholesky)/cholesky | solution.py:65
  378.9 9.8 %custom-call.25 = f32[1,128,128]{1,2,0:T(8,128)S(1)} custom-call(f32[1,128,128]{2,1,0:T(8,128)S(1)} %get-tuple-element.62), custom_call_target="InvertDiagBlocksLowerTriangular" | custom-call | tf_op jit(solution)/shard_map/jit(cholesky)/cholesky | solution.py:65
  388.8 0.2 constant_dynamic-update-slice_fusion
  389.0 0.3 convolution_subtract_fusion.4
  389.3 11.7 %cholesky.181 = f32[128,128]{1,0:T(8,128)S(1)} custom-call(f32[128,128]{1,0:T(8,128)S(1)} %convolution_subtract_fusion.4), custom_call_target="Cholesky" | custom-call | tf_op jit(solution)/shard_map/jit(cholesky)/cholesky | solution.py:65
  401.0 0.6 compare_reduce_fusion.1
  401.7 0.7 compare_reduce_fusion
  403.6 3.9 while.7
  403.6 0.6 fusion.61
  404.2 1.3 bitcast_dynamic-update-slice_fusion.5
  405.6 0.6 fusion.61
  406.2 1.3 bitcast_dynamic-update-slice_fusion.5
  407.5 19.7 %custom-call.26 = f32[2,128,128]{1,2,0:T(8,128)S(1)} custom-call(f32[2,128,128]{2,1,0:T(8,128)S(1)} %get-tuple-element.38), custom_call_target="InvertDiagBlocksLowerTriangular" | custom-call | tf_op jit(solution)/shard_map/jit(_solve_triangular)/triangular_solve | solution.py:12
  427.2 2.0 fusion.1
  429.2 0.5 constant_dynamic-slice_fusion.3
  429.7 1.9 copy.70
  431.7 0.3 fusion.20
  432.0 0.2 convolution_subtract_fusion.7
  432.5 4.6 copy.98
  437.1 1.9 fusion.2
  439.0 2.0 convolution_subtract_fusion
  441.0 1.9 fusion.36
  443.0 0.4 fusion
  443.4 1.0 copy-done.6
  444.4 2.9 convolution_subtract_fusion.3
  447.2 0.5 constant_dynamic-slice_fusion.2
  447.7 2.0 copy.80
  449.7 1.7 copy.78
  451.5 5.5 %pad_maximum_fusion.4 = f32[512,8,1,128]{3,1,0,2:T(8,128)} fusion(f32[512,8,1,64]{3,1,0,2:T(8,128)} %bitcast.154, f32[512,8,1,32]{3,1,0,2:T(8,128)} %bitcast.152, f32[512,8,1,32]{3,1,0,2:T(8,128)} %bitcast.151), kind=kLoop, calls=%fused_computation.18 | loop fusion | flops 1048576 | bytes 4194304 | tf_op jit(solution)/shard_map/concatenate | solution.py:74
  (57 shorter events, 2.5 us)
Async XLA Ops:
  6.5 111.6 %copy-start = (bf16[1024,1024]{1,0:T(8,128)(2,1)S(1)}, bf16[1024,1024]{1,0:T(8,128)(2,1)}, u32[]{:S(2)}) copy-start(bf16[1024,1024]{1,0:T(8,128)(2,1)} %param.6) | copy-start | bytes 6291460
  6.5 111.6 %all-gather.6.cloned.1.call-start = ((), (), s32[]{:S(2)}) async-start(), calls=%async_computation.1 | async-start | bytes 2105344 | tf_op jit(solution)/shard_map/all_gather | solution.py:33
  8.0 291.7 %all-gather.8.cloned.1.call-start = ((), (), s32[]{:S(2)}) async-start(), calls=%async_computation.2 | async-start | bytes 4718592 | tf_op jit(solution)/shard_map/all_gather | solution.py:57
  182.1 1.3 copy-start.3
  184.8 247.6 %all-gather.10.cloned.1.call-start = ((), (), s32[]{:S(2)}) async-start(), calls=%async_computation.3 | async-start | bytes 4718592 | tf_op jit(solution)/shard_map/all_gather | solution.py:57
  184.9 1.9 slice-start
  237.0 59.8 %copy-start.4 = (f32[4096,96]{1,0:T(8,128)S(1)}, f32[4096,96]{1,0:T(8,128)}, u32[]{:S(2)}) copy-start(f32[4096,96]{1,0:T(8,128)} %slice.153) | copy-start | bytes 4718596
  308.3 2.0 copy-start.7
  310.3 2.8 copy-start.2
  313.0 1.1 copy-start.5
  442.9 1.4 copy-start.6
  451.5 5.5 %copy-start.1 = (bf16[1024,1024]{1,0:T(8,128)(2,1)S(1)}, bf16[1024,1024]{1,0:T(8,128)(2,1)}, u32[]{:S(2)}) copy-start(bf16[1024,1024]{1,0:T(8,128)(2,1)} %param.6) | copy-start | bytes 6291460
Sparse Core Ops, SparseCore 0:
  11.1 107.0 all-gather.5
  184.9 53.2 all-gather.7
  315.2 53.6 all-gather.9
where the time goes:
time: 469 us; the launch traced here: 464 us
  blocking collectives  157 us (33%)
  other arithmetic  116 us (25%)
  waiting for transfers between devices  110 us (23%)
  local copies, waits for them, and re-layouts  38.8 us (8%)
  matrix products  25.5 us (5%)
  between operations  16.2 us (3%)
    all_gather x1, waiting for transfers between devices, local(): lax.all_gather(constraint_rows[:panel_depth], ('wide', 'narrow'), axis=1,...  110 us
    another operation x13, other arithmetic, local(): factor_low = jnp.linalg.cholesky(diag_block)  68.6 us
    all_to_all x1, blocking collectives, local(): lax.all_to_all(strip_major(schur_slab, strips), 'narrow', split_axis=2, c...  56.3 us
    all_gather x2, blocking collectives, local(): lax.all_gather(shared[:, :narrow_panel], 'narrow', axis=1, tiled=True)  53.2 us
    all_gather x2, blocking collectives, local(): shared = lax.all_gather(own_rows, 'wide', axis=1, tiled=True)  47 us
    another operation x5, other arithmetic, left_solve(): return jax.scipy.linalg.solve_triangular(factor_low, right_side, lower=True)  39.4 us
    another operation x12, matrix products, left_solve(): return jax.scipy.linalg.solve_triangular(factor_low, right_side, lower=True)  13.2 us
  transfers between devices with their start and end apart: 3, of which 1 were waited for; matrix products, arithmetic and copies ran while one was open for 28% of the time, Pallas kernels for 0%

commit v1 on v0

--- a/solution.py
+++ b/solution.py
@@ -50,7 +50,7 @@
         own_rows = flat_block.reshape(row_count, strips, strip_len)[
             row_begin : row_begin + block_rows, :, strip_begin:
         ]
-        shared = lax.all_gather(own_rows, "wide", axis=1, tiled=True)
+        shared = jnp.concatenate(lax.all_gather(own_rows, "wide"), axis=1)
         shared = shared.reshape(PB, strip_len - strip_begin)
         diag_strip, row_strip = (
             lax.all_gather(shared[:, :narrow_panel], "narrow", axis=1, tiled=True),

time: 469 us -> 471 us (level)
  no operation moved by 1% of the time
where the time goes in v1:
time: 471 us; the launch traced here: 465 us
  blocking collectives  157 us (33%)
  other arithmetic  116 us (25%)
  waiting for transfers between devices  110 us (23%)
  local copies, waits for them, and re-layouts  40.1 us (9%)
  matrix products  25.5 us (5%)
  between operations  16.4 us (3%)
    all_gather x1, waiting for transfers between devices, local(): lax.all_gather(constraint_rows[:panel_depth], ('wide', 'narrow'), axis=1,...  110 us
    another operation x13, other arithmetic, local(): factor_low = jnp.linalg.cholesky(diag_block)  68.7 us
    all_to_all x1, blocking collectives, local(): lax.all_to_all(strip_major(schur_slab, strips), 'narrow', split_axis=2, c...  56.3 us
    all_gather x2, blocking collectives, local(): lax.all_gather(shared[:, :narrow_panel], 'narrow', axis=1, tiled=True)  53.1 us
    all_gather x2, blocking collectives, local(): shared = jnp.concatenate(lax.all_gather(own_rows, 'wide'), axis=1)  47.2 us
    another operation x5, other arithmetic, left_solve(): return jax.scipy.linalg.solve_triangular(factor_low, right_side, lower=True)  39.4 us
    another operation x12, matrix products, left_solve(): return jax.scipy.linalg.solve_triangular(factor_low, right_side, lower=True)  13.2 us
  transfers between devices with their start and end apart: 3, of which 1 were waited for; matrix products, arithmetic and copies ran while one was open for 28% of the time, Pallas kernels for 0%

profile of v1, /device:TPU:4, one launch (start us, length us, event | category | flops | bytes accessed | tf_op | source)
XLA Modules:
  0.0 465.2 jit_solution(17749053667751028280)
XLA Ops:
  6.5 1.5 slice.100
  8.1 110.0 %all-gather.5.cloned.1.call-done = bf16[4,256,1024]{2,0,1:T(4,128)(2,1)} async-done(((bf16[4,1,1024]{2,0,1:T(4,128)(2,1)}), bf16[4,256,1024]{2,0,1:T(4,128)(2,1)}) %all-gather.5.cloned.1.call-update) | async-done | bytes 2097168 | tf_op jit(solution)/shard_map/all_gather | solution.py:33
  118.1 5.7 %fusion.8 = f32[512,4,256]{0,2,1:T(8,128)} fusion(bf16[4,256,1024]{2,0,1:T(4,128)(2,1)} %all-gather.5.cloned.1.call-done, bf16[1024,1024]{1,0:T(8,128)(2,1)S(1)} %copy-done, bf16[512,1,1024]{2,0,1:T(8,128)(2,1)} %param.5), kind=kOutput, calls=%fused_computation.22 | convolution fusion | flops 2148532224 | bytes 7340032 | tf_op jit(solution)/shard_map/rn,kmn->rkm/dot_general | solution.py:30
  123.8 2.0 copy.62
  125.8 56.3 %all_to_all.4 = f32[512,1,8,128]{3,0,1,2:T(8,128)S(1)} all-to-all(f32[512,1,8,128]{3,0,1,2:T(8,128)S(1)} %bitcast.152), channel_id=1, replica_groups=mesh['wide'=32,'narrow'=8] {'narrow'}, dimensions={2} | all-to-all | bytes 4194304 | tf_op jit(solution)/shard_map/all_to_all | solution.py:37
  182.1 1.2 copy.99
  183.4 1.4 copy.68
  184.9 1.9 slice.147
  186.8 0.8 slice.144
  187.6 23.0 %all_gather.26 = f32[32,1,8,128]{3,2,1,0:T(8,128)S(1)} all-gather(f32[1,1,8,128]{3,2,1,0:T(8,128)S(1)} %bitcast.167), channel_id=1, replica_groups=mesh['wide'=32,'narrow'=8] {'wide'}, dimensions={0}, use_global_device_ids=true | all-gather | bytes 135168 | tf_op jit(solution)/shard_map/all_gather | solution.py:53
  210.9 26.6 %all_gather.27 = f32[256,256]{0,1:T(8,128)S(1)} all-gather(f32[256,32]{0,1:T(8,128)S(1)} %copy.64), channel_id=1, replica_groups=mesh['wide'=32,'narrow'=8] {'narrow'}, dimensions={1}, use_global_device_ids=true | all-gather | bytes 294912 | tf_op jit(solution)/shard_map/all_gather | solution.py:56
  238.0 11.7 %cholesky.130 = f32[128,128]{1,0:T(8,128)S(1)} custom-call(f32[128,128]{1,0:T(8,128)S(1)} %cholesky.194), custom_call_target="Cholesky" | custom-call | tf_op jit(solution)/shard_map/jit(cholesky)/cholesky | solution.py:65
  249.7 9.8 %custom-call.23 = f32[1,128,128]{1,2,0:T(8,128)S(1)} custom-call(f32[1,128,128]{2,1,0:T(8,128)S(1)} %get-tuple-element.66), custom_call_target="InvertDiagBlocksLowerTriangular" | custom-call | tf_op jit(solution)/shard_map/jit(cholesky)/cholesky | solution.py:65
  259.6 0.2 constant_dynamic-update-slice_fusion.2
  259.8 0.3 convolution_subtract_fusion.5
  260.1 11.7 %cholesky.147 = f32[128,128]{1,0:T(8,128)S(1)} custom-call(f32[128,128]{1,0:T(8,128)S(1)} %convolution_subtract_fusion.5), custom_call_target="Cholesky" | custom-call | tf_op jit(solution)/shard_map/jit(cholesky)/cholesky | solution.py:65
  271.8 0.7 compare_reduce_fusion.2
  274.0 4.2 while.6
  274.0 0.6 fusion.60
  274.6 1.4 bitcast_dynamic-update-slice_fusion.4
  276.1 0.6 fusion.60
  276.7 1.4 bitcast_dynamic-update-slice_fusion.4
  278.1 19.7 %custom-call.24 = f32[2,128,128]{1,2,0:T(8,128)S(1)} custom-call(f32[2,128,128]{2,1,0:T(8,128)S(1)} %get-tuple-element.37), custom_call_target="InvertDiagBlocksLowerTriangular" | custom-call | tf_op jit(solution)/shard_map/jit(_solve_triangular)/triangular_solve | solution.py:12
  297.8 2.1 copy.82
  299.9 0.3 fusion.24
  300.3 0.3 convolution_subtract_fusion.6
  300.8 4.6 copy.98
  305.4 1.9 fusion.4
  307.3 2.0 convolution_subtract_fusion.1
  309.3 1.9 fusion.34
  311.3 2.7 convolution_subtract_fusion.2
  314.0 1.1 copy-done.5
  315.2 0.9 slice.150
  316.1 0.9 slice.148
  317.0 24.1 %all-gather = f32[256,96]{1,0:T(8,128)S(1)} all-gather(f32[8,96]{1,0:T(8,128)S(1)} %copy.73), channel_id=2, replica_groups=mesh['wide'=32,'narrow'=8] {'wide'}, dimensions={0}, use_global_device_ids=true | all-gather | bytes 101376 | tf_op jit(solution)/shard_map/all_gather | solution.py:53
  341.3 26.5 %all_gather.31 = f32[256,256]{0,1:T(8,128)S(1)} all-gather(f32[256,32]{0,1:T(8,128)S(1)} %copy.84), channel_id=1, replica_groups=mesh['wide'=32,'narrow'=8] {'narrow'}, dimensions={1}, use_global_device_ids=true | all-gather | bytes 294912 | tf_op jit(solution)/shard_map/all_gather | solution.py:56
  368.3 11.7 %cholesky.164 = f32[128,128]{1,0:T(8,128)S(1)} custom-call(f32[128,128]{1,0:T(8,128)S(1)} %cholesky.197), custom_call_target="Cholesky" | custom-call | tf_op jit(solution)/shard_map/jit(cholesky)/cholesky | solution.py:65
  380.1 9.8 %custom-call.25 = f32[1,128,128]{1,2,0:T(8,128)S(1)} custom-call(f32[1,128,128]{2,1,0:T(8,128)S(1)} %get-tuple-element.62), custom_call_target="InvertDiagBlocksLowerTriangular" | custom-call | tf_op jit(solution)/shard_map/jit(cholesky)/cholesky | solution.py:65
  390.1 0.3 convolution_subtract_fusion.4
  390.4 11.7 %cholesky.181 = f32[128,128]{1,0:T(8,128)S(1)} custom-call(f32[128,128]{1,0:T(8,128)S(1)} %convolution_subtract_fusion.4), custom_call_target="Cholesky" | custom-call | tf_op jit(solution)/shard_map/jit(cholesky)/cholesky | solution.py:65
  402.1 0.7 compare_reduce_fusion.1
  402.8 0.7 compare_reduce_fusion
  404.9 4.1 while.7
  404.9 0.6 fusion.61
  405.5 1.4 bitcast_dynamic-update-slice_fusion.5
  406.9 0.6 fusion.61
  407.6 1.4 bitcast_dynamic-update-slice_fusion.5
  409.0 19.7 %custom-call.26 = f32[2,128,128]{1,2,0:T(8,128)S(1)} custom-call(f32[2,128,128]{2,1,0:T(8,128)S(1)} %get-tuple-element.38), custom_call_target="InvertDiagBlocksLowerTriangular" | custom-call | tf_op jit(solution)/shard_map/jit(_solve_triangular)/triangular_solve | solution.py:12
  428.7 2.0 fusion.1
  430.7 0.5 constant_dynamic-slice_fusion.3
  431.2 2.0 copy.70
  433.2 0.3 fusion.20
  433.5 0.2 convolution_subtract_fusion.7
  434.0 4.6 copy.97
  438.6 1.9 fusion.2
  440.5 2.0 convolution_subtract_fusion
  442.5 1.9 fusion.36
  444.5 0.4 fusion
  444.9 1.0 copy-done.6
  445.9 2.9 convolution_subtract_fusion.3
  448.8 0.5 constant_dynamic-slice_fusion.2
  449.3 1.9 copy.80
  451.2 1.7 copy.78
  452.9 5.5 %pad_maximum_fusion.4 = f32[512,8,1,128]{3,1,0,2:T(8,128)} fusion(f32[512,8,1,64]{3,1,0,2:T(8,128)} %bitcast.153, f32[512,8,1,32]{3,1,0,2:T(8,128)} %bitcast.151, f32[512,8,1,32]{3,1,0,2:T(8,128)} %bitcast.150), kind=kLoop, calls=%fused_computation.18 | loop fusion | flops 1048576 | bytes 4194304 | tf_op jit(solution)/shard_map/concatenate | solution.py:74
  (56 shorter events, 2.7 us)
Async XLA Ops:
  6.5 111.6 %copy-start = (bf16[1024,1024]{1,0:T(8,128)(2,1)S(1)}, bf16[1024,1024]{1,0:T(8,128)(2,1)}, u32[]{:S(2)}) copy-start(bf16[1024,1024]{1,0:T(8,128)(2,1)} %param.6) | copy-start | bytes 6291460
  6.5 111.6 %all-gather.5.cloned.1.call-start = ((), (), s32[]{:S(2)}) async-start(), calls=%async_computation.1 | async-start | bytes 2105344 | tf_op jit(solution)/shard_map/all_gather | solution.py:33
  8.0 292.7 %all-gather.7.cloned.1.call-start = ((), (), s32[]{:S(2)}) async-start(), calls=%async_computation.2 | async-start | bytes 4718592 | tf_op jit(solution)/shard_map/all_gather | solution.py:57
  182.1 1.3 copy-start.3
  184.8 249.1 %all-gather.9.cloned.1.call-start = ((), (), s32[]{:S(2)}) async-start(), calls=%async_computation.3 | async-start | bytes 4718592 | tf_op jit(solution)/shard_map/all_gather | solution.py:57
  237.6 60.2 %copy-start.4 = (f32[4096,96]{1,0:T(8,128)S(1)}, f32[4096,96]{1,0:T(8,128)}, u32[]{:S(2)}) copy-start(f32[4096,96]{1,0:T(8,128)} %slice.147) | copy-start | bytes 4718596
  309.3 2.0 copy-start.7
  311.3 2.8 copy-start.2
  314.0 1.1 copy-start.5
  444.5 1.4 copy-start.6
  452.9 5.5 %copy-start.1 = (bf16[1024,1024]{1,0:T(8,128)(2,1)S(1)}, bf16[1024,1024]{1,0:T(8,128)(2,1)}, u32[]{:S(2)}) copy-start(bf16[1024,1024]{1,0:T(8,128)(2,1)} %param.6) | copy-start | bytes 6291460
Sparse Core Ops, SparseCore 0:
  11.1 107.0 all-gather.4
  184.9 53.2 all-gather.6
  316.2 53.7 all-gather.8
